TPU v7x, 256 devices: a whole 4x4x8 slice. The times are simulated.
256 devices in a mesh: cam: 8 (over x, core), clip: 32 (over y, z).
Axes of the slice: x: 4, y: 4, z: 8, core: 2. Of those that a mesh axis runs over, the one named last changes fastest.
Arguments:
- tokens: bfloat16 [64, 8, 256, 1024], P('clip', 'cam'), may hold values from -6 to 6
- w_query: bfloat16 [1024, 1024], replicated, may hold values from -0.1875 to 0.1875
- w_key: bfloat16 [1024, 1024], replicated, may hold values from -0.1875 to 0.1875
- w_value: bfloat16 [1024, 1024], replicated, may hold values from -0.1875 to 0.1875
- w_proj: bfloat16 [1024, 256], replicated, may hold values from -0.1875 to 0.1875
- prototypes: bfloat16 [256, 65536], P(None, ('cam', 'clip')), may hold values from -6 to 6
Outputs:
- codes: float32 [64, 65536], P(None, ('cam', 'clip'))
- prototype_gradient: float32 [256, 65536], P(None, ('cam', 'clip'))
- grad_proj: float32 [1024, 256], P('clip')
- grad_value: float32 [1024, 1024], P('clip', 'cam')
All inputs are finite; a program needn't handle non-finite values.
Results may differ from a plain program's by a relative error of at most 0.015.
Values may be sent and summed in bfloat16 or wider, within the bound.
A program may use at most 128 MiB of HBM per device.

v0:
```python
import jax
import jax.numpy as jnp
from jax import lax
from jax.sharding import PartitionSpec as P

D = 1024
HD = 64
PROTOS = 65536
TOK = 256
ITERS = 3
H = 16
SINK_EPS = 0.05
SOFTMAX_TEMP = 0.1
NORM_EPS = 1e-06
heads_per_group = 4


def column_sums(query_rows, key_rows, total):
    scores = jnp.einsum(
        "ihe,jhe->hij", query_rows, key_rows, preferred_element_type=jnp.float32
    ) * HD ** (-0.5)
    exponent_values = jnp.exp(scores)
    probs = exponent_values / jnp.sum(exponent_values, axis=2, keepdims=True)
    return jnp.sum(probs, axis=1) / total


def camera_block(query_clip, key_clip, total):
    tokens_here = query_clip.shape[0]
    width = heads_per_group * HD
    parts = []
    for group in range(H // heads_per_group):
        query_group = query_clip[:, group * width : (group + 1) * width].reshape(
            tokens_here, heads_per_group, HD
        )
        key_group = key_clip[:, group * width : (group + 1) * width].reshape(
            total, heads_per_group, HD
        )
        parts.append(column_sums(query_group, key_group, total))
    return jnp.concatenate(parts, axis=0)


def local(tokens, w_query, w_key, w_value, w_proj, prototypes):
    clips = tokens.shape[0]
    own = tokens.reshape(clips, TOK, D)
    query_vectors = jnp.einsum(
        "ctd,de->cte", own, w_query, preferred_element_type=jnp.float32
    ).astype(jnp.bfloat16)
    key_rows = jnp.einsum("ctd,de->cte", own, w_key, preferred_element_type=jnp.float32).astype(
        jnp.bfloat16
    )
    collected_rows = lax.all_gather(key_rows.reshape(clips, 1, TOK, D), "cam", axis=1, tiled=True)
    cameras = collected_rows.shape[1]
    total = cameras * TOK

    def per_clip(clip_pair):
        return camera_block(clip_pair[0], clip_pair[1], total)

    partial_sums = lax.map(per_clip, (query_vectors, collected_rows.reshape(clips, total, D)))
    weights = lax.psum_scatter(
        partial_sums.reshape(clips, H, cameras, TOK), "cam", scatter_dimension=2, tiled=True
    )
    weights = weights.reshape(clips, H, TOK).astype(jnp.bfloat16)
    mixture = jnp.einsum("chj,cjd->chd", weights, own, preferred_element_type=jnp.float32).astype(
        jnp.bfloat16
    )
    head_out = jnp.einsum(
        "chd,dhe->che", mixture, w_value.reshape(D, H, HD), preferred_element_type=jnp.float32
    )
    pooled = lax.psum(head_out.reshape(clips, D), "cam").astype(jnp.bfloat16)
    share_rows = D // lax.axis_size("clip")
    embed = jnp.dot(pooled, w_proj, preferred_element_type=jnp.float32)
    embed_norm = jnp.sqrt(jnp.sum(embed * embed, axis=1, keepdims=True) + NORM_EPS)
    unit = embed / embed_norm
    unit_b = unit.astype(jnp.bfloat16)
    all_units = lax.all_gather(unit_b, "clip", axis=0, tiled=True)
    proto_f = prototypes.astype(jnp.float32)
    column_norm = jnp.sqrt(jnp.sum(proto_f * proto_f, axis=0, keepdims=True) + NORM_EPS)
    unit_proto = proto_f / column_norm
    proto_b = unit_proto.astype(jnp.bfloat16)
    logit_scores = jnp.dot(all_units, proto_b, preferred_element_type=jnp.float32)
    exponent_values = jnp.exp(logit_scores / SOFTMAX_TEMP)
    assign = jnp.exp(logit_scores / SINK_EPS)
    prob_total = lax.psum(jnp.sum(exponent_values, axis=1), ("cam", "clip"))
    first_step = 0
    for step in range(first_step, ITERS):
        assign = assign / jnp.sum(assign, axis=0, keepdims=True)
        row_total = lax.psum(jnp.sum(assign, axis=1), ("cam", "clip"))
        assign = assign / row_total[:, None]
    prob = exponent_values / prob_total[:, None]
    grad_logits = (PROTOS * (prob - assign)).astype(jnp.bfloat16)
    codes = PROTOS * assign
    grad_unit = lax.psum_scatter(
        jnp.dot(grad_logits, proto_b.T, preferred_element_type=jnp.float32),
        "clip",
        scatter_dimension=0,
        tiled=True,
    )
    grad_unit = lax.psum(grad_unit, "cam")
    grad_embed = (grad_unit - unit * jnp.sum(unit * grad_unit, axis=1, keepdims=True)) / embed_norm
    grad_embed_b = grad_embed.astype(jnp.bfloat16)
    grad_pooled = jnp.dot(grad_embed_b, w_proj.T, preferred_element_type=jnp.float32).astype(
        jnp.bfloat16
    )
    piece = pooled
    grad_proj = lax.psum_scatter(
        jnp.einsum("cd,ce->de", piece, grad_embed_b, preferred_element_type=jnp.float32),
        "clip",
        scatter_dimension=0,
        tiled=True,
    )
    grad_heads = grad_pooled.reshape(clips, H, HD)
    piece = lax.slice_in_dim(mixture, 0, share_rows * lax.axis_size("clip"), axis=2)
    value_rows = lax.psum_scatter(
        jnp.einsum("chd,che->dhe", piece, grad_heads, preferred_element_type=jnp.float32).reshape(
            share_rows * lax.axis_size("clip"), D
        ),
        "clip",
        scatter_dimension=0,
        tiled=True,
    )
    grad_value = lax.psum_scatter(value_rows, "cam", scatter_dimension=1, tiled=True)
    grad_unit_proto = jnp.einsum(
        "be,bk->ek", all_units, grad_logits, preferred_element_type=jnp.float32
    )
    prototype_gradient = (
        grad_unit_proto - unit_proto * jnp.sum(unit_proto * grad_unit_proto, axis=0, keepdims=True)
    ) / column_norm
    return (codes, prototype_gradient, grad_proj, grad_value)


def solution(mesh):
    in_specs = (P("clip", "cam", None, None), P(), P(), P(), P(), P(None, ("cam", "clip")))
    out_specs = (
        P(None, ("cam", "clip")),
        P(None, ("cam", "clip")),
        P("clip", None),
        P("clip", "cam"),
    )
    return jax.shard_map(local, mesh=mesh, in_specs=in_specs, out_specs=out_specs, check_vma=False)
```

profile of v0, /device:TPU:8, one launch (start us, length us, event | category | flops | bytes accessed | tf_op | source)
XLA Modules:
  0.0 1159.4 jit_solution(2229369669846176685)
XLA Ops:
  20.2 47.3 %all-gather.4.cloned.1.call-done = bf16[2,2048,1024]{2,1,0:T(8,128)(2,1)} async-done(((bf16[2,256,1024]{2,1,0:T(8,128)(2,1)}), bf16[2,2048,1024]{2,1,0:T(8,128)(2,1)}) %all-gather.4.cloned.1.call-update) | async-done | bytes 8388624 | tf_op jit(solution)/shard_map/all_gather | solution.py:51
  67.5 130.2 %while.10 = (s32[]{:T(128)}, f32[2,16,2048]{2,1,0:T(8,128)}, bf16[2,256,1024]{2,1,0:T(8,128)(2,1)}, bf16[2,2048,1024]{2,1,0:T(8,128)(2,1)}, s32[]{:T(128)}) while((s32[]{:T(128)}, f32[2,16,2048]{2,1,0:T(8,128)}, bf16[2,256,1024]{2,1,0:T(8,128)(2,1)}, bf16[2,2048,1024]{2,1,0:T(8,128)(2,1)}, s32[]{:T(128)}) %tuple.47), condition=%wide.region_9.10_spmd, body=%wide.region_0.9_spmd.sunk | while | flops 2181148672 | bytes 112328888 | solution.py:58
  67.5 4.6 constant_dynamic-slice_fusion.6
  72.1 6.5 copy.50
  87.1 5.7 fusion.143
  92.9 7.5 divide_reduce_fusion.11
  104.8 6.1 divide_reduce_fusion.12
  111.8 4.5 fusion.142
  116.3 5.5 divide_reduce_fusion.10
  121.8 4.5 fusion.141
  126.3 5.6 divide_reduce_fusion.9
  132.7 4.6 constant_dynamic-slice_fusion.6
  137.3 6.5 copy.50
  152.3 5.7 fusion.143
  158.0 7.5 divide_reduce_fusion.11
  169.9 6.1 divide_reduce_fusion.12
  176.9 4.5 fusion.142
  181.4 5.5 divide_reduce_fusion.10
  186.9 4.5 fusion.141
  191.4 5.6 divide_reduce_fusion.9
  201.4 31.9 %reduce-scatter.5.cloned.1.call-done = f32[2,16,1,256]{3,1,0,2:T(8,128)} async-done(((f32[2,16,8,256]{3,1,0,2:T(8,128)}), f32[2,16,1,256]{3,1,0,2:T(8,128)}) %reduce-scatter.5.cloned.1.call-update) | async-done | bytes 32784 | tf_op jit(solution)/shard_map/reduce_scatter | solution.py:59
  237.1 13.2 %psum.42 = bf16[2,1024]{1,0:T(2,128)(2,1)S(1)} all-reduce(f32[2,1024]{1,0:T(2,128)S(1)} %reshape.88), channel_id=1, replica_groups=mesh['cam'=8,'clip'=32] {'cam'}, use_global_device_ids=true, to_apply=%region_11.12 | all-reduce | flops 2048 | bytes 12288 | tf_op jit(solution)/shard_map/psum | solution.py:69
  251.7 43.0 %all-gather.1 = bf16[32,2,256]{2,1,0:T(2,128)(2,1)S(1)} all-gather(bf16[1,2,256]{2,1,0:T(2,128)(2,1)S(1)} %get-tuple-element.51), channel_id=1, replica_groups=mesh['cam'=8,'clip'=32] {'clip'}, dimensions={0}, use_global_device_ids=true | all-gather | bytes 33792 | tf_op jit(solution)/shard_map/all_gather | solution.py:75
  295.1 72.7 %psum.43 = f32[64]{0:T(128)S(1)} all-reduce(f32[64]{0:T(128)S(1)} %get-tuple-element.40), channel_id=1, replica_groups=mesh['cam'=8,'clip'=32] {'cam','clip'}, use_global_device_ids=true, to_apply=%region_16.17 | all-reduce | flops 64 | bytes 512 | tf_op jit(solution)/shard_map/psum | solution.py:87
  368.0 74.3 %psum.44 = f32[64]{0:T(128)S(1)} all-reduce(f32[64]{0:T(128)S(1)} %fusion.48), channel_id=1, replica_groups=mesh['cam'=8,'clip'=32] {'cam','clip'}, use_global_device_ids=true, to_apply=%region_19.20 | all-reduce | flops 64 | bytes 512 | tf_op jit(solution)/shard_map/psum | solution.py:87
  442.6 73.4 %all-reduce.1 = (f32[64]{0:T(128)S(1)}, f32[64]{0:T(128)S(1)}) all-reduce(f32[64]{0:T(128)S(1)} %fusion.50, f32[64]{0:T(128)S(1)} %get-tuple-element.39), channel_id=1, replica_groups=mesh['cam'=8,'clip'=32] {'cam','clip'}, use_global_device_ids=true, to_apply=%region_22.23 | all-reduce | flops 128 | bytes 1024 | tf_op jit(solution)/shard_map/psum | solution.py:87
  518.8 137.5 %all-reduce.4.cloned.1.call-done = f32[64,256]{1,0:T(8,128)} async-done(((f32[64,256]{1,0:T(8,128)}), f32[64,256]{1,0:T(8,128)}) %all-reduce.4.cloned.1.call-update) | async-done | bytes 65552
  657.1 12.4 %psum.47 = f32[2,256]{1,0:T(2,128)S(1)} all-reduce(f32[2,256]{1,0:T(2,128)S(1)} %constant_dynamic-slice_fusion.2), channel_id=1, replica_groups=mesh['cam'=8,'clip'=32] {'cam'}, use_global_device_ids=true, to_apply=%region_27.28 | all-reduce | flops 512 | bytes 4096 | tf_op jit(solution)/shard_map/psum | solution.py:98
  673.7 5.4 copy.35
  680.6 217.1 %reduce-scatter.9.cloned.1.call-done = f32[32,1024]{1,0:T(8,128)} async-done(((f32[1024,1024]{1,0:T(8,128)}), f32[32,1024]{1,0:T(8,128)}) %reduce-scatter.9.cloned.1.call-update) | async-done | bytes 131088 | tf_op jit(solution)/shard_map/reduce_scatter | solution.py:113
  898.7 218.6 %reduce-scatter.7.cloned.1.call-done = f32[32,256]{1,0:T(8,128)} async-done(((f32[1024,256]{1,0:T(8,128)}), f32[32,256]{1,0:T(8,128)}) %reduce-scatter.7.cloned.1.call-update) | async-done | bytes 32784 | tf_op jit(solution)/shard_map/reduce_scatter | solution.py:105
  1117.3 35.2 %reduce-scatter.11.cloned.1.call-done = f32[32,128]{1,0:T(8,128)} async-done(((f32[32,1024]{1,0:T(8,128)}), f32[32,128]{1,0:T(8,128)}) %reduce-scatter.11.cloned.1.call-update) | async-done | bytes 16400 | tf_op jit(solution)/shard_map/reduce_scatter | solution.py:121
  (87 shorter events, 61.5 us)
Async XLA Ops:
  7.2 1.6 copy-start
  7.2 9.2 copy-start.5
  7.2 60.4 %all-gather.4.cloned.1.call-start = ((), (), s32[]{:S(2)}) async-start(), calls=%async_computation.8 | async-start | bytes 9437184 | tf_op jit(solution)/shard_map/all_gather | solution.py:51
  12.3 221.0 %reduce-scatter.5.cloned.1.call-start = ((), (), s32[]{:S(2)}) async-start(), calls=%async_computation.4 | async-start | bytes 294912 | tf_op jit(solution)/shard_map/reduce_scatter | solution.py:59
  67.5 450.1 %copy-start.8 = (u32[256]{0:T(256)S(1)}, u32[256]{0:T(256)}, u32[]{:S(2)}) copy-start(u32[256]{0:T(256)} %constant.40) | copy-start | bytes 3076
  78.6 3.8 copy-start.3
  86.5 0.6 copy-start.2
  126.3 5.6 copy-start.6
  132.0 0.7 copy-start.7
  143.7 3.8 copy-start.3
  151.6 0.6 copy-start.2
  191.4 5.6 copy-start.6
  197.1 0.7 copy-start.7
  199.5 456.9 %all-reduce.4.cloned.1.call-start = ((), (), s32[]{:S(2)}) async-start(), calls=%async_computation.9 | async-start | bytes 131072
  517.5 380.1 %reduce-scatter.9.cloned.1.call-start = ((), (), s32[]{:S(2)}) async-start(), calls=%async_computation.6 | async-start | bytes 4325376 | tf_op jit(solution)/shard_map/reduce_scatter | solution.py:113
  671.0 481.5 %copy-start.1 = (bf16[1024,1024]{1,0:T(8,128)(2,1)S(1)}, bf16[1024,1024]{1,0:T(8,128)(2,1)}, u32[]{:S(2)}) copy-start(bf16[1024,1024]{1,0:T(8,128)(2,1)} %param.10) | copy-start | bytes 6291460
  673.7 224.0 %copy-start.4 = (bf16[256,256]{1,0:T(8,128)(2,1)S(1)}, bf16[256,256]{1,0:T(8,128)(2,1)}, u32[]{:S(2)}) copy-start(bf16[256,256]{1,0:T(8,128)(2,1)} %param.13) | copy-start | bytes 393220
  679.1 438.2 %reduce-scatter.7.cloned.1.call-start = ((), (), s32[]{:S(2)}) async-start(), calls=%async_computation.5 | async-start | bytes 1081344 | tf_op jit(solution)/shard_map/reduce_scatter | solution.py:105
  680.5 472.0 %reduce-scatter.11.cloned.1.call-start = ((), (), s32[]{:S(2)}) async-start(), calls=%async_computation.7 | async-start | bytes 147456 | tf_op jit(solution)/shard_map/reduce_scatter | solution.py:121
Sparse Core Ops, SparseCore 0:
  12.5 55.0 all-gather.3
  199.6 33.6 reduce-scatter.4
  517.7 138.6 all-reduce.3
  679.3 218.3 reduce-scatter.8
  901.9 215.3 reduce-scatter.6
  1120.2 32.2 reduce-scatter.10
where the time goes:
time: 1160 us
  waiting for transfers between devices  688 us (59%)
  blocking collectives  289 us (25%)
  matrix products  107 us (9%)
  local copies, waits for them, and re-layouts  54.6 us (5%)
  between operations  14.9 us (1%)
    psum x3, blocking collectives, local(): row_total = lax.psum(jnp.sum(assign, axis=1), ('cam', 'clip'))  220 us
    reduce_scatter x1, waiting for transfers between devices, local(): lax.psum_scatter(jnp.einsum('cd,ce->de', piece, grad_embed_b, preferred_e...  219 us
    reduce_scatter x1, waiting for transfers between devices, local(): lax.psum_scatter(jnp.einsum('chd,che->dhe', piece, grad_heads, preferred_...  217 us
    unnamed x7, waiting for transfers between devices  138 us
    div x8, matrix products, column_sums(): probs = exponent_values / jnp.sum(exponent_values, axis=2, keepdims=True)  49.5 us
    all_gather x1, waiting for transfers between devices, local(): lax.all_gather(key_rows.reshape(clips, 1, TOK, D), 'cam', axis=1, tiled=T...  47.3 us
    all_gather x1, blocking collectives, local(): all_units = lax.all_gather(unit_b, 'clip', axis=0, tiled=True)  43 us
    dot_general x8, matrix products, column_sums(): jnp.einsum('ihe,jhe->hij', query_rows, key_rows, preferred_element_type=j...  38.4 us
  transfers between devices with their start and end apart: 6, of which 6 were waited for; matrix products, arithmetic and copies ran while one was open for 1% of the time, Pallas kernels for 0%

commit v1 on v0

--- a/solution.py
+++ b/solution.py
@@ -13,6 +13,11 @@
 SOFTMAX_TEMP = 0.1
 NORM_EPS = 1e-06
 heads_per_group = 4
+
+
+def add_all(x, mesh_axis):
+    terms = lax.all_gather(x, mesh_axis)
+    return jnp.sum(terms, axis=0)
 
 
 def column_sums(query_rows, key_rows, total):
@@ -84,7 +89,7 @@
     first_step = 0
     for step in range(first_step, ITERS):
         assign = assign / jnp.sum(assign, axis=0, keepdims=True)
-        row_total = lax.psum(jnp.sum(assign, axis=1), ("cam", "clip"))
+        row_total = add_all(jnp.sum(assign, axis=1), ("cam", "clip"))
         assign = assign / row_total[:, None]
     prob = exponent_values / prob_total[:, None]
     grad_logits = (PROTOS * (prob - assign)).astype(jnp.bfloat16)

time: 1160 us -> 1670 us (1.44)
  waiting for transfers between devices: 688 us -> 1340 us
  blocking collectives: 289 us -> 143 us
    unnamed x7 -> x13, waiting for transfers between devices: 138 us -> 786 us
    psum x3 -> x1, blocking collectives: 220 us -> 74.3 us  [local(): prob_total = lax.psum(jnp.sum(exponent_values, axis=1), ('cam', 'clip'))]
  transfers between devices with their start and end apart: 6 -> 9, of which waited for: 6 -> 9; matrix products, arithmetic and copies ran while one was open for 1% -> 1% of each run, Pallas kernels for 0% -> 0%
where the time goes in v1:
time: 1670 us
  waiting for transfers between devices  1340 us (80%)
  blocking collectives  143 us (9%)
  matrix products  107 us (6%)
  local copies, waits for them, and re-layouts  60.1 us (4%)
    unnamed x13, waiting for transfers between devices  786 us
    reduce_scatter x1, waiting for transfers between devices, local(): lax.psum_scatter(jnp.einsum('cd,ce->de', piece, grad_embed_b, preferred_e...  219 us
    reduce_scatter x1, waiting for transfers between devices, local(): lax.psum_scatter(jnp.einsum('chd,che->dhe', piece, grad_heads, preferred_...  217 us
    psum x1, blocking collectives, local(): prob_total = lax.psum(jnp.sum(exponent_values, axis=1), ('cam', 'clip'))  74.3 us
    div x8, matrix products, column_sums(): probs = exponent_values / jnp.sum(exponent_values, axis=2, keepdims=True)  49.5 us
    all_gather x1, waiting for transfers between devices, local(): lax.all_gather(key_rows.reshape(clips, 1, TOK, D), 'cam', axis=1, tiled=T...  47.3 us
    all_gather x1, blocking collectives, local(): all_units = lax.all_gather(unit_b, 'clip', axis=0, tiled=True)  43 us
    dot_general x8, matrix products, column_sums(): jnp.einsum('ihe,jhe->hij', query_rows, key_rows, preferred_element_type=j...  38.4 us
  transfers between devices with their start and end apart: 9, of which 9 were waited for; matrix products, arithmetic and copies ran while one was open for 1% of the time, Pallas kernels for 0%

profile of v1, /device:TPU:8, one launch (start us, length us, event | category | flops | bytes accessed | tf_op | source)
XLA Modules:
  0.0 1667.2 jit_solution(16680891827759426276)
XLA Ops:
  20.2 47.3 %all-gather.7.cloned.1.call-done = bf16[2,2048,1024]{2,1,0:T(8,128)(2,1)} async-done(((bf16[2,256,1024]{2,1,0:T(8,128)(2,1)}), bf16[2,2048,1024]{2,1,0:T(8,128)(2,1)}) %all-gather.7.cloned.1.call-update) | async-done | bytes 8388624 | tf_op jit(solution)/shard_map/all_gather | solution.py:56
  67.5 130.2 %while.10 = (s32[]{:T(128)}, f32[2,16,2048]{2,1,0:T(8,128)}, bf16[2,256,1024]{2,1,0:T(8,128)(2,1)}, bf16[2,2048,1024]{2,1,0:T(8,128)(2,1)}, s32[]{:T(128)}) while((s32[]{:T(128)}, f32[2,16,2048]{2,1,0:T(8,128)}, bf16[2,256,1024]{2,1,0:T(8,128)(2,1)}, bf16[2,2048,1024]{2,1,0:T(8,128)(2,1)}, s32[]{:T(128)}) %tuple.47), condition=%wide.region_9.10_spmd, body=%wide.region_0.9_spmd.sunk | while | flops 2181148672 | bytes 112328888 | solution.py:63
  67.5 4.6 constant_dynamic-slice_fusion.6
  72.1 6.5 copy.50
  87.1 5.7 fusion.143
  92.9 7.5 divide_reduce_fusion.11
  104.8 6.1 divide_reduce_fusion.12
  111.8 4.5 fusion.142
  116.3 5.5 divide_reduce_fusion.10
  121.8 4.5 fusion.141
  126.3 5.6 divide_reduce_fusion.9
  132.7 4.6 constant_dynamic-slice_fusion.6
  137.3 6.5 copy.50
  152.3 5.7 fusion.143
  158.0 7.5 divide_reduce_fusion.11
  169.9 6.1 divide_reduce_fusion.12
  176.9 4.5 fusion.142
  181.4 5.5 divide_reduce_fusion.10
  191.4 5.6 divide_reduce_fusion.9
  201.4 31.9 %reduce-scatter.5.cloned.1.call-done = f32[2,16,1,256]{3,1,0,2:T(8,128)} async-done(((f32[2,16,8,256]{3,1,0,2:T(8,128)}), f32[2,16,1,256]{3,1,0,2:T(8,128)}) %reduce-scatter.5.cloned.1.call-update) | async-done | bytes 32784 | tf_op jit(solution)/shard_map/reduce_scatter | solution.py:64
  237.1 13.2 psum.21
  251.7 43.0 %all-gather.4 = bf16[32,2,256]{2,1,0:T(2,128)(2,1)S(1)} all-gather(bf16[1,2,256]{2,1,0:T(2,128)(2,1)S(1)} %get-tuple-element.49), channel_id=1, replica_groups=mesh['cam'=8,'clip'=32] {'clip'}, dimensions={0}, use_global_device_ids=true | all-gather | bytes 33792 | tf_op jit(solution)/shard_map/all_gather | solution.py:80
  296.1 237.6 %all-reduce.9.cloned.1.call-done = f32[16384]{0:T(1024)} async-done(((f32[16384]{0:T(1024)}), f32[16384]{0:T(1024)}) %all-reduce.9.cloned.1.call-update) | async-done | bytes 65552
  535.9 241.6 %all-reduce.11.cloned.1.call-done = f32[16384]{0:T(1024)} async-done(((f32[16384]{0:T(1024)}), f32[16384]{0:T(1024)}) %all-reduce.11.cloned.1.call-update) | async-done | bytes 65552
  779.7 74.3 %psum.22 = f32[64]{0:T(128)S(1)} all-reduce(f32[64]{0:T(128)S(1)} %get-tuple-element.39), channel_id=1, replica_groups=mesh['cam'=8,'clip'=32] {'cam','clip'}, use_global_device_ids=true, to_apply=%region_24.25 | all-reduce | flops 64 | bytes 512 | tf_op jit(solution)/shard_map/psum | solution.py:88
  854.0 167.7 %all-reduce.13.cloned.1.call-done = f32[16384]{0:T(1024)} async-done(((f32[16384]{0:T(1024)}), f32[16384]{0:T(1024)}) %all-reduce.13.cloned.1.call-update) | async-done | bytes 65552
  1025.5 138.8 %all-reduce.15.cloned.1.call-done = f32[64,256]{1,0:T(8,128)} async-done(((f32[64,256]{1,0:T(8,128)}), f32[64,256]{1,0:T(8,128)}) %all-reduce.15.cloned.1.call-update) | async-done | bytes 65552
  1165.0 12.4 psum.23
  1181.6 5.4 copy.35
  1188.5 216.9 %reduce-scatter.9.cloned.1.call-done = f32[32,1024]{1,0:T(8,128)} async-done(((f32[1024,1024]{1,0:T(8,128)}), f32[32,1024]{1,0:T(8,128)}) %reduce-scatter.9.cloned.1.call-update) | async-done | bytes 131088 | tf_op jit(solution)/shard_map/reduce_scatter | solution.py:118
  1406.5 218.7 %reduce-scatter.7.cloned.1.call-done = f32[32,256]{1,0:T(8,128)} async-done(((f32[1024,256]{1,0:T(8,128)}), f32[32,256]{1,0:T(8,128)}) %reduce-scatter.7.cloned.1.call-update) | async-done | bytes 32784 | tf_op jit(solution)/shard_map/reduce_scatter | solution.py:110
  1625.1 35.5 %reduce-scatter.11.cloned.1.call-done = f32[32,128]{1,0:T(8,128)} async-done(((f32[32,1024]{1,0:T(8,128)}), f32[32,128]{1,0:T(8,128)}) %reduce-scatter.11.cloned.1.call-update) | async-done | bytes 16400 | tf_op jit(solution)/shard_map/reduce_scatter | solution.py:126
  (112 shorter events, 71.8 us)
Async XLA Ops:
  7.2 1.6 copy-start
  7.2 9.2 copy-start.5
  7.2 60.4 %all-gather.7.cloned.1.call-start = ((), (), s32[]{:S(2)}) async-start(), calls=%async_computation.8 | async-start | bytes 9437184 | tf_op jit(solution)/shard_map/all_gather | solution.py:56
  12.3 221.0 %reduce-scatter.5.cloned.1.call-start = ((), (), s32[]{:S(2)}) async-start(), calls=%async_computation.4 | async-start | bytes 294912 | tf_op jit(solution)/shard_map/reduce_scatter | solution.py:64
  67.5 956.7 %copy-start.11 = (u32[256]{0:T(256)S(1)}, u32[256]{0:T(256)}, u32[]{:S(2)}) copy-start(u32[256]{0:T(256)} %constant.52) | copy-start | bytes 3076
  78.6 3.8 copy-start.3
  86.5 0.6 copy-start.2
  126.3 5.6 copy-start.6
  132.0 0.7 copy-start.7
  143.7 3.8 copy-start.3
  151.6 0.6 copy-start.2
  191.4 5.6 copy-start.6
  197.1 0.7 copy-start.7
  199.5 334.1 %all-reduce.9.cloned.1.call-start = ((), (), s32[]{:S(2)}) async-start(), calls=%async_computation.9 | async-start | bytes 131072
  295.4 0.6 copy-start.9
  296.0 481.5 %all-reduce.11.cloned.1.call-start = ((), (), s32[]{:S(2)}) async-start(), calls=%async_computation.10 | async-start | bytes 131072
  535.2 0.6 copy-start.10
  535.8 485.8 %all-reduce.13.cloned.1.call-start = ((), (), s32[]{:S(2)}) async-start(), calls=%async_computation.11 | async-start | bytes 131072
  779.0 0.6 copy-start.8
  779.7 384.6 %all-reduce.15.cloned.1.call-start = ((), (), s32[]{:S(2)}) async-start(), calls=%async_computation.12 | async-start | bytes 131072
  1024.2 381.2 %reduce-scatter.9.cloned.1.call-start = ((), (), s32[]{:S(2)}) async-start(), calls=%async_computation.6 | async-start | bytes 4325376 | tf_op jit(solution)/shard_map/reduce_scatter | solution.py:118
  1178.9 481.8 %copy-start.1 = (bf16[1024,1024]{1,0:T(8,128)(2,1)S(1)}, bf16[1024,1024]{1,0:T(8,128)(2,1)}, u32[]{:S(2)}) copy-start(bf16[1024,1024]{1,0:T(8,128)(2,1)} %param.10) | copy-start | bytes 6291460
  1181.6 223.8 %copy-start.4 = (bf16[256,256]{1,0:T(8,128)(2,1)S(1)}, bf16[256,256]{1,0:T(8,128)(2,1)}, u32[]{:S(2)}) copy-start(bf16[256,256]{1,0:T(8,128)(2,1)} %param.13) | copy-start | bytes 393220
  1187.1 438.1 %reduce-scatter.7.cloned.1.call-start = ((), (), s32[]{:S(2)}) async-start(), calls=%async_computation.5 | async-start | bytes 1081344 | tf_op jit(solution)/shard_map/reduce_scatter | solution.py:110
  1188.5 472.2 %reduce-scatter.11.cloned.1.call-start = ((), (), s32[]{:S(2)}) async-start(), calls=%async_computation.7 | async-start | bytes 147456 | tf_op jit(solution)/shard_map/reduce_scatter | solution.py:126
Sparse Core Ops, SparseCore 0:
  12.5 55.0 all-gather.6
  199.6 33.6 reduce-scatter.4
  296.1 237.4 all-reduce.8
  539.6 237.8 all-reduce.10
  783.4 238.2 all-reduce.12
  1025.6 138.6 all-reduce.14
  1187.2 218.2 reduce-scatter.8
  1409.8 215.2 reduce-scatter.6
  1628.2 32.4 reduce-scatter.10
